TPU v7x, 32 devices: a whole 2x2x4 slice. The times are simulated.
32 devices in a mesh: gx: 8 (over z, x), gy: 4 (over y, core).
Axes of the slice: x: 2, y: 2, z: 4, core: 2. Of those that a mesh axis runs over, the one named last changes fastest.
Arguments:
- velocity: float32 [3, 64, 256, 128], P(None, 'gx', 'gy'), may hold values from -2 to 3, as said below
- counts: int32 [8, 4, 9], P('gx', 'gy'), may hold values from 1 to 1024, as said below
- src_cell: int32 [8, 4, 9, 1024], P('gx', 'gy'), may hold values from 0 to 65535
- weights: float32 [8, 4, 9, 1024], P('gx', 'gy'), may hold values from 0.05 to 0.35
- dst_cell: int32 [8, 4, 9, 1024], P('gx', 'gy'), may hold values from 0 to 65535
- blade_tile: int32 [20, 192], replicated, may hold values from 0 to 31, as said below
- blade_cell: int32 [20, 192], replicated, may hold values from 0 to 65535
- blade_coef: float32 [20, 192], replicated, may hold values from 0.5 to 2
Outputs:
- updated: float32 [3, 64, 256, 128], P(None, 'gx', 'gy')
- forcing: float32 [3, 64, 256, 128], P(None, 'gx', 'gy')
Inputs may be any that keep to these rules, and one draw needn't show every extreme that they name: The velocity components, streamwise with a mean near 1. `counts`: some list is full, with 1024 used slots. `blade_tile`: turbines stand near one spanwise row of tiles; a turbine's points lie in at most three tiles.
All inputs are finite; a program needn't handle non-finite values.
Results may differ from a plain program's by a relative error of at most 0.00002.
Values sent between devices are 32-bit elements; how exact they have to be, the bound alone decides.
No kernel may reach another device: no remote copies, remote signals or barrier semaphores. Data moves between devices by JAX's collectives and lax.ppermute only.
A program may use at most 256 MiB of HBM per device.

v0:
```python
import jax
import jax.numpy as jnp
from jax import lax
from jax.experimental import pallas as pl
from jax.experimental.pallas import tpu as pltpu
from jax.sharding import PartitionSpec as P

F32 = jnp.float32
BF16 = jnp.bfloat16
VMEM = pl.BlockSpec(memory_space=pltpu.VMEM)
SMEM = pl.BlockSpec(memory_space=pltpu.SMEM)
HBM = pl.BlockSpec(memory_space=pltpu.HBM)


def halves(value):
    high = value.astype(BF16)
    low = (value - high.astype(F32)).astype(BF16)
    return high, low


def one_hot(extent, index):
    rows = lax.broadcasted_iota(jnp.int32, (extent, index.shape[1]), 0)
    return jnp.where(rows == index, 1.0, 0.0).astype(BF16)


def pick(table, cell):
    key = (cell & 127) | (((cell >> 15) & 1) << 7)
    place = (cell >> 7) & 255
    hot = one_hot(256, key)
    hot = jnp.concatenate([hot, hot], axis=0)
    here = lax.broadcasted_iota(jnp.int32, (256, cell.shape[1]), 0) == place
    out = []
    for c in range(3):
        found = jnp.dot(table[c], hot, preferred_element_type=F32)
        out.append(jnp.sum(jnp.where(here, found, 0.0), axis=0, keepdims=True))
    return out


def spread(extent, row, level, values):
    hot = one_hot(extent, row)
    at_level = lax.broadcasted_iota(jnp.int32, (128, level.shape[1]), 0) == level
    high, low = [], []
    for value in values:
        vh = value.astype(BF16).astype(F32)
        high.append(jnp.where(at_level, vh, 0.0).astype(BF16))
        low.append(jnp.where(at_level, value - vh, 0.0).astype(BF16))
    left = jnp.concatenate([hot, hot], axis=1)
    right = jnp.concatenate([jnp.concatenate(high, axis=0), jnp.concatenate(low, axis=0)], axis=1)
    return lax.dot_general(left, right, (((1,), (1,)), ((), ())), preferred_element_type=F32)


def sides(mine_ref, count_y):
    mine = mine_ref[0]
    return 1 - 2 * ((mine // count_y) & 1), 1 - 2 * (mine & 1)


def list_blocks(lists, listed):
    total = jnp.int32(0)
    for used, tag in lists:
        for j in range(8):
            listed[total + j] = tag * 8 + j
        total = total + ((used + 127) >> 7)
    return total


def run_chunks(total, large, small, chunk):
    many = (total + small - 1) // large

    def big(i, carry):
        chunk(i * large, large)
        return carry

    lax.fori_loop(0, many, big, 0)

    def rest(i, carry):
        chunk(many * large + i * small, small)
        return carry

    lax.fori_loop(0, jnp.maximum(total - many * large + small - 1, 0) // small, rest, 0)


def gather_lists(table, total, large, small, listed, direction, src_ref, w_ref, out_ref):
    for k in range(large):
        listed[total + k] = listed[total - 1]

    def chunk(first, width):
        blocks = [listed[first + k] for k in range(width)]
        rows = [direction[b >> 3] * 8 + (b & 7) for b in blocks]
        cell = jnp.concatenate([src_ref[pl.ds(r, 1), :] for r in rows], axis=1)
        found = pick(table, cell)
        for k, (b, r) in enumerate(zip(blocks, rows)):
            j = b & 7
            weight = w_ref[pl.ds(r, 1), :]
            for c in range(3):
                out_ref[b >> 3, c, pl.ds(j, 1), :] = found[c][:, k * 128 : (k + 1) * 128] * weight
            out_ref[b >> 3, 3, pl.ds(j, 1), :] = weight

    run_chunks(total, large, small, chunk)


def make_far_gather(count_y, large, small):
    def kernel(
        mine_ref, cnt_hbm, vel_hbm, src_hbm, w_hbm, dst_hbm, tile_hbm, cell_hbm, coef_hbm,
        out_ref, table, vel_ref, src_ref, w_ref, dst_ref, tile_ref, cell_ref, coef_ref, pts_ref, rot_ref,
        sem, cnt_ref, listed, direction, tlist,
    ):
        half = vel_ref.shape[1] // 2
        pairs = [(cnt_hbm, cnt_ref), (src_hbm, src_ref), (w_hbm, w_ref), (tile_hbm, tile_ref)]
        pairs += [(vel_hbm.at[c], vel_ref.at[c]) for c in range(3)]
        pairs += [(cell_hbm, cell_ref), (coef_hbm, coef_ref), (dst_hbm, dst_ref)]
        copies = [pltpu.make_async_copy(a, b, sem.at[k]) for k, (a, b) in enumerate(pairs)]
        for copy in copies:
            copy.start()
        out_ref[...] = jnp.zeros_like(out_ref)
        pts_ref[...] = jnp.zeros_like(pts_ref)
        for copy in copies[:4]:
            copy.wait()
        n_turb = active_turbines(tile_ref, mine_ref[0], tlist)
        slot = lax.broadcasted_iota(jnp.int32, (8, 128), 0) * 128 + lax.broadcasted_iota(jnp.int32, (8, 128), 1)
        for d in range(9):
            part = slice(d * 8, d * 8 + 8)
            w_ref[part, :] = jnp.where(slot < cnt_ref[0, 0, d], w_ref[part, :], 0.0)
        side_x, side_y = sides(mine_ref, count_y)
        lists = []
        for s in range(2):
            for t in range(3):
                d = 3 * (side_x * (1 - 2 * s) + 1) + side_y * (1 - t) + 1
                direction[3 * s + t] = d
                lists.append((cnt_ref[0, 0, d], 3 * s + t))
        total = list_blocks(lists, listed)
        for c in range(3):
            copies[4 + c].wait()
            for piece in range(2):
                high, low = halves(vel_ref[c, piece * half : (piece + 1) * half, :])
                table[c, :, piece * 128 : (piece + 1) * 128] = high
                table[c, :, 256 + piece * 128 : 256 + (piece + 1) * 128] = low
        for copy in copies[7:]:
            copy.wait()
        gather_lists(table, total, large, small, listed, direction, src_ref, w_ref, out_ref)
        gather_points(mine_ref[0], n_turb, table, tile_ref, cell_ref, pts_ref, rot_ref, tlist)

    return kernel


def active_turbines(tile_ref, mine, listed):
    turbines = tile_ref.shape[0]
    owned = jnp.where(tile_ref[...] == mine, 1.0, 0.0)
    found = jnp.max(owned, axis=1, keepdims=True)
    total = jnp.int32(0)
    for t in range(turbines):
        listed[total] = t
        total = total + jnp.where(found[t, 0] > 0.5, 1, 0)
    listed[total] = 0
    return total


def diagonal(turbines):
    shape = (turbines, 128)
    return lax.broadcasted_iota(jnp.int32, shape, 0) == lax.broadcasted_iota(jnp.int32, shape, 1)


def gather_points(mine, n_turb, table, tile_ref, cell_ref, pts_ref, rot_ref, tlist):
    turbines, points = tile_ref.shape

    def turbine(i, carry):
        pair = [tlist[2 * i], tlist[2 * i + 1]]
        cell = jnp.concatenate([cell_ref[pl.ds(t, 1), :] for t in pair], axis=1)
        found = pick(table, cell)
        for k, t in enumerate(pair):
            owned = tile_ref[pl.ds(t, 1), :] == mine
            for c in range(3):
                pts_ref[c, pl.ds(t, 1), :] = jnp.where(owned, found[c][:, k * points : (k + 1) * points], 0.0)
        return carry

    lax.fori_loop(0, (n_turb + 1) >> 1, turbine, 0)
    sums = jnp.broadcast_to(jnp.sum(pts_ref[0], axis=1, keepdims=True), (turbines, 128))
    row = jnp.sum(jnp.where(diagonal(turbines), sums, 0.0), axis=0, keepdims=True)
    rot_ref[...] = jnp.broadcast_to(row, rot_ref.shape)


def used_slots(weight):
    return jnp.sum(jnp.where(weight != 0.0, 1.0, 0.0)).astype(jnp.int32)


def make_near_gather(count_y, large, small):
    def kernel(mine_ref, table, src_ref, w_ref, dst_ref, out_ref, acc, listed, direction):
        out_ref[...] = jnp.zeros_like(out_ref)
        acc[...] = jnp.zeros_like(acc)
        _, side_y = sides(mine_ref, count_y)
        used = [used_slots(w_ref[d * 8 : d * 8 + 8, :]) for d in (3, 4, 5)]
        last = jnp.where(side_y > 0, used[0], used[2])
        lists = [(jnp.where(side_y > 0, used[2], used[0]), 0), (used[1], 1), (last, 2)]
        for t in range(3):
            direction[t] = 3 + side_y * (1 - t) + 1
        total = list_blocks(lists, listed)
        gather_lists(table, total, large, small, listed, direction, src_ref, w_ref, out_ref)
        direction[0] = 4
        scatter_lists(out_ref.at[1:2], 1, direction, dst_ref, listed, acc, 512, lambda row: row, 8, 4)

    return kernel


def scatter_lists(val, n_lists, direction, dst_ref, listed, acc, extent, place, large, small):
    lists = []
    for q in range(n_lists):
        lists.append((used_slots(val[q, 3]), q))
    total = list_blocks(lists, listed)
    for k in range(large):
        listed[total + k] = 0

    def chunk(first, width):
        cells, vals = [], [[], [], [], []]
        for k in range(width):
            b = listed[first + k]
            q, j = b >> 3, b & 7
            keep = jnp.where(first + k < total, 1.0, 0.0)
            cells.append(dst_ref[pl.ds(direction[q] * 8 + j, 1), :])
            for c in range(4):
                vals[c].append(val[q, c, pl.ds(j, 1), :] * keep)
        cell = jnp.concatenate(cells, axis=1)
        vals = [jnp.concatenate(v, axis=1) for v in vals]
        acc[...] += spread(extent, place((cell >> 7) & 511), cell & 127, vals)

    run_chunks(total, large, small, chunk)


def load_level_lists(side_x, low_ref, high_ref, start, val, direction):
    for q, ref in enumerate((low_ref, high_ref)):
        for c in range(4):
            val[start + q, c] = ref[32 + c * 8 : 40 + c * 8, :]
        direction[start + q] = 3 * (side_x * (2 * q - 1) + 1) + 1


def make_level_edges(count_y):
    def kernel(mine_ref, base_ref, low_ref, high_ref, dst_ref, edge, val, listed, direction):
        side_x, _ = sides(mine_ref, count_y)
        load_level_lists(side_x, low_ref, high_ref, 0, val, direction)
        edge[...] = edge_rows(base_ref, None, slice(None))
        scatter_lists(val, 2, direction, dst_ref, listed, edge, 144, edge_place, 12, 4)

    return kernel


def make_core_edges(count_y):
    def kernel(mine_ref, base_ref, first_ref, dst_ref, edge, val, listed, direction):
        side_x, side_y = sides(mine_ref, count_y)
        load_later_lists(side_x, -side_y, first_ref, 0, val, direction)
        edge[...] = base_ref[...]
        scatter_lists(val, 3, direction, dst_ref, listed, edge, 144, edge_place, 12, 4)

    return kernel


def load_later_lists(side_x, from_y, ref, start, val, direction):
    for s in range(3):
        for c in range(4):
            at = (s * 4 + c) * 8
            val[start + s, c] = ref[at : at + 8, :]
        direction[start + s] = 3 * (side_x * (s - 1) + 1) + from_y + 1


def corrected(acc, vel, c):
    return (1.0 - acc[:, 384:512]) * vel - acc[:, c * 128 : (c + 1) * 128]


def edge_rows(ref, c, columns):
    at = (lambda r: ref[r, columns]) if c is None else (lambda r: ref[c, r, columns])
    spare = [at(slice(0, 2))]
    low = [at(slice(x * 64, x * 64 + 1)) for x in range(1, 7)]
    high = [at(slice(x * 64 + 63, x * 64 + 64)) for x in range(1, 7)]
    return jnp.concatenate([at(slice(0, 64)), at(slice(448, 512))] + low + spare + high + spare, axis=0)


def edge_place(row):
    x, y = row >> 6, row & 63
    inside = jnp.where(y == 0, 127 + x, jnp.where(y == 63, 135 + x, 1024))
    return jnp.where(x == 0, y, jnp.where(x == 7, 64 + y, inside))


def make_edge_scatter(count_y):
    def kernel(
        mine_ref, base_ref, second_ref, dst_ref, vel_ref,
        cor_ref, xa_ref, xb_ref, ya_ref, yb_ref, acc, val, listed, direction,
    ):
        side_x, side_y = sides(mine_ref, count_y)
        load_later_lists(side_x, side_y, second_ref, 0, val, direction)
        acc[...] = base_ref[...]
        scatter_lists(val, 3, direction, dst_ref, listed, acc, 144, edge_place, 12, 4)
        for c in range(3):
            cor = corrected(acc, edge_rows(vel_ref, c, slice(None)), c)
            cor_ref[c] = cor[0:128]
            xa_ref[c] = jnp.where(side_x > 0, cor[64:128], cor[0:64])
            xb_ref[c] = jnp.where(side_x > 0, cor[0:64], cor[64:128])
            low = jnp.concatenate([cor[0:1], cor[128:134], cor[64:65]], axis=0)
            high = jnp.concatenate([cor[63:64], cor[136:142], cor[127:128]], axis=0)
            ya_ref[c] = jnp.where(side_y > 0, high, low)
            yb_ref[c] = jnp.where(side_y > 0, low, high)

    return kernel


def make_inner_scatter(count_y):
    def kernel(mine_ref, base_ref, low_ref, high_ref, first_ref, second_ref, dst_ref, vel_ref, cor_ref, acc, val, listed, direction):
        side_x, side_y = sides(mine_ref, count_y)
        load_later_lists(side_x, -side_y, first_ref, 0, val, direction)
        load_later_lists(side_x, side_y, second_ref, 3, val, direction)
        load_level_lists(side_x, low_ref, high_ref, 6, val, direction)
        acc[...] = base_ref[64:448, :]
        scatter_lists(val, 8, direction, dst_ref, listed, acc, 384, lambda row: row - 64, 12, 4)
        for c in range(3):
            cor_ref[c] = corrected(acc, vel_ref[c, 64:448, :], c)

    return kernel


def add_forces(mine, tile_ref, cell_ref, coef_ref, pts_ref, rot_ref, column, out_ref, tlist):
    out_ref[...] = jnp.zeros_like(out_ref)
    turbines = tile_ref.shape[0]
    sums = jnp.broadcast_to(rot_ref[0:1, :], (turbines, 128))
    sums = jnp.sum(jnp.where(diagonal(turbines), sums, 0.0), axis=1, keepdims=True)
    column[...] = jnp.broadcast_to(sums, (turbines, 128))
    n_turb = active_turbines(tile_ref, mine, tlist)
    points = tile_ref.shape[1]

    def turbine(i, carry):
        pair = [tlist[2 * i], tlist[2 * i + 1]]
        cell = jnp.concatenate([cell_ref[pl.ds(t, 1), :] for t in pair], axis=1)
        force = [[], [], []]
        for k, t in enumerate(pair):
            keep = jnp.where(2 * i + k < n_turb, 1.0 / points, 0.0)
            scale = -coef_ref[pl.ds(t, 1), :] * (column[pl.ds(t, 1), 0:1] * keep)
            for c in range(3):
                force[c].append(scale * pts_ref[c, pl.ds(t, 1), :])
        force = [jnp.concatenate(f, axis=1) for f in force]
        got = spread(512, (cell >> 7) & 511, cell & 127, force)
        for c in range(3):
            out_ref[c] += got[:, c * 128 : (c + 1) * 128]
        return carry

    lax.fori_loop(0, (n_turb + 1) >> 1, turbine, 0)


def make_stencil(count_y):
    def kernel(
        mine_ref, edge_ref, inner_ref, tile_ref, cell_ref, coef_ref, pts_ref, rot_ref, xa_ref, xb_ref, ya_ref, yb_ref,
        out_hbm, frc_hbm, out_ref, frc_ref, column, sem, tlist,
    ):
        add_forces(mine_ref[0], tile_ref, cell_ref, coef_ref, pts_ref, rot_ref, column, frc_ref, tlist)
        given = pltpu.make_async_copy(frc_ref, frc_hbm, sem.at[8])
        given.start()
        side_x, side_y = sides(mine_ref, count_y)
        lane = lax.broadcasted_iota(jnp.int32, (64, 128), 1)

        def slab(c, x):
            if x < 0:
                return jnp.where(side_x > 0, xb_ref[c * 64 : c * 64 + 64, :], xa_ref[c * 64 : c * 64 + 64, :])
            if x > 7:
                return jnp.where(side_x > 0, xa_ref[c * 64 : c * 64 + 64, :], xb_ref[c * 64 : c * 64 + 64, :])
            ref, at = (inner_ref, x - 1) if 1 <= x < 7 else (edge_ref, 0 if x == 0 else 1)
            return ref[c, at * 64 : at * 64 + 64, :]

        copies = []
        for x in range(8):
            now = [slab(c, x) for c in range(3)]
            up = [0.03 - 0.1 * v for v in now]
            down = [0.03 + 0.1 * v for v in now]
            up[2] = jnp.where(lane == 127, 0.0, up[2])
            down[2] = jnp.where(lane == 0, 0.0, down[2])
            for c in range(3):
                u = now[c]
                west, east = slab(c, x - 1), slab(c, x + 1)
                ya, yb = ya_ref[c, x : x + 1, :], yb_ref[c, x : x + 1, :]
                south = jnp.concatenate([jnp.where(side_y > 0, yb, ya), u[:-1]], axis=0)
                north = jnp.concatenate([u[1:], jnp.where(side_y > 0, ya, yb)], axis=0)
                upper, lower = pltpu.roll(u, 127, 1), pltpu.roll(u, 1, 1)
                moved = (up[0] * east + down[0] * west) + (up[1] * north + down[1] * south)
                moved = moved + (up[2] * upper + down[2] * lower)
                out_ref[c, x] = 0.82 * u + (moved + 0.2 * frc_ref[c, x * 64 : x * 64 + 64, :])
            copies.append(pltpu.make_async_copy(out_ref.at[:, x], out_hbm.at[:, x], sem.at[x]))
            copies[-1].start()
        for copy in copies:
            copy.wait()
        given.wait()

    return kernel


def swap(value, axis, step):
    count = lax.axis_size(axis)
    return lax.ppermute(value, axis, [(i, i ^ step) for i in range(count)])


def swap_next(value, axis):
    count = lax.axis_size(axis)
    return lax.ppermute(value, axis, [(i, (i - 1 if i % 2 == 0 else i + 1) % count) for i in range(count)])


def call(kernel, name, outs, ins, args, scratch=(), flops=10**9, limit=32):
    return pl.pallas_call(
        kernel,
        out_shape=tuple(jax.ShapeDtypeStruct(shape, dtype) for shape, dtype, _ in outs),
        in_specs=ins,
        out_specs=tuple(spec for _, _, spec in outs),
        scratch_shapes=list(scratch),
        compiler_params=pltpu.CompilerParams(vmem_limit_bytes=limit << 20),
        cost_estimate=pl.CostEstimate(flops=flops, bytes_accessed=10**5, transcendentals=0),
        name=name,
    )(*args)


def body(velocity, counts, src_cell, weights, dst_cell, blade_tile, blade_cell, blade_coef):
    vel = velocity.reshape(3, 512, 128)
    src = src_cell.reshape(72, 128)
    weight = weights.reshape(72, 128)
    dst = dst_cell.reshape(72, 128)
    turbines, points = blade_cell.shape
    count_x, count_y = lax.axis_size("gx"), lax.axis_size("gy")
    mine = (lax.axis_index("gx") * count_y + lax.axis_index("gy")).reshape(1).astype(jnp.int32)
    ints = lambda n: pltpu.SMEM((n,), jnp.int32)

    whole = ((72, 128), jnp.int32, VMEM)
    ints_t = (blade_tile.shape, jnp.int32, VMEM)
    given = (counts, vel, src, weight, dst, blade_tile, blade_cell, blade_coef)
    far, table, vel, src, weight, dst, tile, cell, coef, pts, rotor = call(
        make_far_gather(count_y, 12, 4),
        "far_gather",
        [((6, 4, 8, 128), F32, VMEM), ((3, 256, 512), BF16, VMEM), ((3, 512, 128), F32, VMEM), whole]
        + [((72, 128), F32, VMEM), whole, ints_t, ints_t, (blade_tile.shape, F32, VMEM)]
        + [((3, turbines, points), F32, VMEM), ((8, 128), F32, VMEM)],
        [SMEM] + [HBM] * 8,
        (mine,) + tuple(pltpu.with_memory_space_constraint(v, pltpu.HBM) for v in given),
        [pltpu.SemaphoreType.DMA((10,)), pltpu.SMEM((1, 1, 9), jnp.int32), ints(72), ints(8), ints(32)],
        flops=5 * 10**9,
    )
    low = swap(jnp.concatenate([far[0:3].reshape(96, 128), rotor], axis=0), "gx", 1)
    high = swap_next(far[3:6].reshape(96, 128), "gx")
    own, acc = call(
        make_near_gather(count_y, 8, 4),
        "near_gather",
        [((3, 4, 8, 128), F32, VMEM), ((512, 512), F32, VMEM)],
        [SMEM] + [VMEM] * 4,
        (mine, table, src, weight, dst),
        [ints(48), ints(8)],
        flops=4 * 10**9,
    )
    rotor = rotor + low[96:]
    own = own.reshape(96, 128)

    def y_payload(t):
        return jnp.concatenate([part[t * 32 : t * 32 + 32] for part in (low, own, high)] + [rotor], axis=0)

    first = swap(y_payload(0), "gy", 1)
    rotor = rotor + first[96:]
    second = swap_next(y_payload(2), "gy")
    (edge,) = call(
        make_level_edges(count_y),
        "level_edges",
        [((144, 512), F32, VMEM)],
        [SMEM] + [VMEM] * 4,
        (mine, acc, low, high, dst),
        [pltpu.VMEM((2, 4, 8, 128), F32), ints(48), ints(8)],
        flops=4 * 10**9,
    )
    (edge,) = call(
        make_core_edges(count_y),
        "core_edges",
        [((144, 512), F32, VMEM)],
        [SMEM] + [VMEM] * 3,
        (mine, edge, first, dst),
        [pltpu.VMEM((3, 4, 8, 128), F32), ints(48), ints(8)],
        flops=4 * 10**9,
    )
    rotor = rotor + second[96:]
    for axis, count in (("gx", count_x), ("gy", count_y)):
        step = 4
        while step < count:
            rotor = rotor + swap(rotor, axis, step)
            step *= 2
    lists = pltpu.VMEM((8, 4, 8, 128), F32)
    face_x, face_y = ((3, 64, 128), F32, VMEM), ((3, 8, 128), F32, VMEM)
    edge, xa, xb, ya, yb = call(
        make_edge_scatter(count_y),
        "edge_scatter",
        [((3, 128, 128), F32, VMEM), face_x, face_x, face_y, face_y],
        [SMEM] + [VMEM] * 4,
        (mine, edge, second, dst, vel),
        [pltpu.VMEM((144, 512), F32), pltpu.VMEM((3, 4, 8, 128), F32), ints(48), ints(8)],
        flops=4 * 10**9,
    )
    xb = swap_next(jnp.concatenate([xb.reshape(192, 128), rotor], axis=0), "gx")
    xa = swap(xa.reshape(192, 128), "gx", 1)
    ya = swap(ya, "gy", 1)
    yb = swap_next(yb, "gy")
    (inner,) = call(
        make_inner_scatter(count_y),
        "inner_scatter",
        [((3, 384, 128), F32, VMEM)],
        [SMEM] + [VMEM] * 7,
        (mine, acc, low, high, first, second, dst, vel),
        [pltpu.VMEM((384, 512), F32), lists, ints(96), ints(8)],
        flops=6 * 10**9,
    )
    rotor = rotor + xb[192:]
    updated, forcing = call(
        make_stencil(count_y),
        "stencil",
        [((3, 8, 64, 128), F32, HBM), ((3, 512, 128), F32, HBM)],
        [SMEM] + [VMEM] * 11,
        (mine, edge, inner, tile, cell, coef, pts, rotor, xa, xb, ya, yb),
        [pltpu.VMEM((3, 8, 64, 128), F32), pltpu.VMEM((3, 512, 128), F32), pltpu.VMEM((turbines, 128), F32)]
        + [pltpu.SemaphoreType.DMA((9,)), ints(32)],
    )
    return updated, forcing.reshape(velocity.shape)


def solution(mesh):
    grid = P("gx", "gy", None)
    lists = P("gx", "gy", None, None)
    field = P(None, "gx", "gy", None)
    return jax.shard_map(
        body,
        mesh=mesh,
        in_specs=(field, grid, lists, lists, lists, P(), P(), P()),
        out_specs=(field, field),
        check_vma=False,
    )
```

profile of v0, /device:TPU:0, one launch (start us, length us, event | category | flops | bytes accessed | tf_op | source)
XLA Modules:
  0.0 38.9 jit_solution(2775476516369313048)
XLA Ops:
  0.6 6.1 %far_gather.1 = (f32[6,4,8,128]{3,2,1,0:T(8,128)S(1)}, bf16[3,256,512]{2,1,0:T(8,128)(2,1)S(1)}, f32[3,512,128]{2,1,0:T(8,128)S(1)}, s32[72,128]{1,0:T(8,128)S(1...) custom-call(s32[1]{0:T(128)} %bitcast.mine_ref, ...), custom_call_target="tpu_custom_call" | custom-call | flops 5000000000 | bytes 100000 | tf_op jit(solution)/shard_map/far_gather/pallas_call | solution.py:399
  6.7 6.0 %collective-permute-start.1 = (f32[96,128]{1,0:T(8,128)S(1)}, f32[96,128]{1,0:T(8,128)S(1)}, u32[]{:S(2)}, u32[]{:S(2)}) collective-permute-start(f32[96,128]{1,0:T(8,128)S(1)} %bitcast.17), channel_id=1, source_target_pairs={{0,28},{4,8},{8,4},{12,16},{16,12},{20,24},{24,20},{28,0},{1,29},{... | collective-permute-start | bytes 147464 | tf_op jit(solution)/shard_map/ppermute | solution.py:395
  12.8 0.9 %collective-permute-start = (f32[104,128]{1,0:T(8,128)S(1)}, f32[104,128]{1,0:T(8,128)S(1)}, u32[]{:S(2)}, u32[]{:S(2)}) collective-permute-start(f32[104,128]{1,0:T(8,128)S(1)} %pad_maximum_fusion.1), channel_id=1, source_target_pairs={{0,4},{4,0},{8,12},{12,8},{16,20},{20,16},{24,28},{28,24},{1,5},{5... | collective-permute-start | bytes 159752 | tf_op jit(solution)/shard_map/ppermute | solution.py:390
  13.6 2.8 %near_gather.1 = (f32[3,4,8,128]{3,2,1,0:T(8,128)S(1)}, f32[512,512]{1,0:T(8,128)S(1)}) custom-call(s32[1]{0:T(128)} %bitcast.mine_ref, bf16[3,256,512]{2,1,0:T(8,128)(2,1)S(1)} %get-tuple-element.22.table, s32[72,128]{1,0:T(8,128)S(1)} %get-tuple-element.23.src_ref, f32[72,128]{1,0:T(8,128)S(1)} %get-tuple-element.24.w_ref, ...), custom_call_target="tpu_custom_call" | custom-call | flops 4000000000 | bytes 100000 | tf_op jit(solution)/shard_map/near_gather/pallas_call | solution.py:399
  16.5 0.0 collective-permute-done.1.high_ref
  16.5 0.4 %collective-permute-done.low_ref = f32[104,128]{1,0:T(8,128)S(1)} collective-permute-done((f32[104,128]{1,0:T(8,128)S(1)}, f32[104,128]{1,0:T(8,128)S(1)}, u32[]{:S(2)}, u32[]{:S(2)}) %collective-permute-start) | collective-permute-done | bytes 53280 | tf_op jit(solution)/shard_map/ppermute | solution.py:390
  16.9 0.1 collective-permute-start.2
  17.0 1.3 %level_edges.1.base_ref = f32[144,512]{1,0:T(8,128)S(1)} custom-call(s32[1]{0:T(128)} %bitcast.mine_ref, f32[512,512]{1,0:T(8,128)S(1)} %get-tuple-element.26.base_ref, f32[104,128]{1,0:T(8,128)S(1)} %collective-permute-done.low_ref, f32[96,128]{1,0:T(8,128)S(1)} %collective-permute-done.1.high_ref, s32[72,128]{1,0:T(8,128)S(1)} %get-tuple-element.25.dst_ref), custom_call_target="tpu_custom_call" | custom-call | flops 4000000000 | bytes 100000 | tf_op jit(solution)/shard_map/level_edges/pallas_call | solution.py:399
  18.4 0.0 collective-permute-done.2.first_ref
  18.4 1.7 %collective-permute-start.3 = (f32[104,128]{1,0:T(8,128)S(1)}, f32[104,128]{1,0:T(8,128)S(1)}, u32[]{:S(2)}, u32[]{:S(2)}) collective-permute-start(f32[104,128]{1,0:T(8,128)S(1)} %pad_maximum_fusion.3), channel_id=1, source_target_pairs={{0,3},{1,2},{2,1},{3,0},{4,7},{5,6},{6,5},{7,4},{8,11},{9,10},{10,... | collective-permute-start | bytes 159752 | tf_op jit(solution)/shard_map/ppermute | solution.py:395
  20.1 1.8 %core_edges.1.base_ref = f32[144,512]{1,0:T(8,128)S(1)} custom-call(s32[1]{0:T(128)} %bitcast.mine_ref, f32[144,512]{1,0:T(8,128)S(1)} %level_edges.1.base_ref, f32[104,128]{1,0:T(8,128)S(1)} %collective-permute-done.2.first_ref, s32[72,128]{1,0:T(8,128)S(1)} %get-tuple-element.25.dst_ref), custom_call_target="tpu_custom_call" | custom-call | flops 4000000000 | bytes 100000 | tf_op jit(solution)/shard_map/core_edges/pallas_call | solution.py:399
  21.9 0.2 collective-permute-done.3.second_ref
  22.1 2.0 %collective-permute-start.4 = (f32[8,128]{1,0:T(8,128)S(1)}, f32[8,128]{1,0:T(8,128)S(1)}, u32[]{:S(2)}, u32[]{:S(2)}) collective-permute-start(f32[8,128]{1,0:T(8,128)S(1)} %slice_add_fusion.1), channel_id=1, source_target_pairs={{0,16},{4,20},{8,24},{12,28},{16,0},{20,4},{24,8},{28,12},{1,17},{... | collective-permute-start | bytes 12296 | tf_op jit(solution)/shard_map/ppermute | solution.py:390
  24.1 1.9 %edge_scatter.1 = (f32[3,128,128]{2,1,0:T(8,128)S(1)}, f32[3,64,128]{2,1,0:T(8,128)S(1)}, f32[3,64,128]{2,1,0:T(8,128)S(1)}, f32[3,8,128]{2,1,0:T(8,128)S(1)}, f32[3,8,128]{2,1,0:T(8,128)S(1)}) custom-call(s32[1]{0:T(128)} %bitcast.mine_ref, f32[144,512]{1,0:T(8,128)S(1)} %core_edges.1.base_ref, f32[104,128]{1,0:T(8,128)S(1)} %collective-permute-done.3.second_ref, ...), custom_call_target="tpu_custom_call" | custom-call | flops 4000000000 | bytes 100000 | tf_op jit(solution)/shard_map/edge_scatter/pallas_call | solution.py:399
  26.0 0.2 collective-permute-start.7
  26.2 0.1 collective-permute-start.8
  26.3 2.3 %collective-permute-start.6 = (f32[192,128]{1,0:T(8,128)S(1)}, f32[192,128]{1,0:T(8,128)S(1)}, u32[]{:S(2)}, u32[]{:S(2)}) collective-permute-start(f32[192,128]{1,0:T(8,128)S(1)} %bitcast.15), channel_id=1, source_target_pairs={{0,4},{4,0},{8,12},{12,8},{16,20},{20,16},{24,28},{28,24},{1,5},{5... | collective-permute-start | bytes 294920 | tf_op jit(solution)/shard_map/ppermute | solution.py:390
  28.6 0.0 collective-permute-done.4
  28.6 2.0 %collective-permute-start.5 = (f32[200,128]{1,0:T(8,128)S(1)}, f32[200,128]{1,0:T(8,128)S(1)}, u32[]{:S(2)}, u32[]{:S(2)}) collective-permute-start(f32[200,128]{1,0:T(8,128)S(1)} %pad_maximum_fusion), channel_id=1, source_target_pairs={{0,28},{4,8},{8,4},{12,16},{16,12},{20,24},{24,20},{28,0},{1,29},{... | collective-permute-start | bytes 307208 | tf_op jit(solution)/shard_map/ppermute | solution.py:395
  30.6 5.8 %inner_scatter.1.inner_ref = f32[3,384,128]{2,1,0:T(8,128)S(1)} custom-call(s32[1]{0:T(128)} %bitcast.mine_ref, f32[512,512]{1,0:T(8,128)S(1)} %get-tuple-element.26.base_ref, f32[104,128]{1,0:T(8,128)S(1)} %collective-permute-done.low_ref, f32[96,128]{1,0:T(8,128)S(1)} %collective-permute-done.1.high_ref, f32[104,128]{1,0:T(8,128)S(1)} %collective-permute-done.2.first_ref, ...), custom_call_target="tpu_custom_call" | custom-call | flops 6000000000 | bytes 100000 | tf_op jit(solution)/shard_map/inner_scatter/pallas_call | solution.py:399
  36.4 0.0 collective-permute-done.5.xb_ref
  36.5 0.0 collective-permute-done.7.ya_ref
  36.5 0.0 collective-permute-done.8.yb_ref
  36.5 0.0 collective-permute-done.6.xa_ref
  36.5 2.4 %stencil.1 = (f32[3,8,64,128]{3,2,1,0:T(8,128)}, f32[3,512,128]{2,1,0:T(8,128)}) custom-call(s32[1]{0:T(128)} %bitcast.mine_ref, f32[3,128,128]{2,1,0:T(8,128)S(1)} %get-tuple-element.31.edge_ref, f32[3,384,128]{2,1,0:T(8,128)S(1)} %inner_scatter.1.inner_ref, s32[20,192]{1,0:T(8,128)S(1)} %get-tuple-element.32.tile_ref, ...), custom_call_target="tpu_custom_call" | custom-call | flops 1000000000 | bytes 100000 | tf_op jit(solution)/shard_map/stencil/pallas_call | solution.py:399
  (13 shorter events, 0.1 us)
Async XLA Ops:
  6.7 9.7 %collective-permute-start.1 = (f32[96,128]{1,0:T(8,128)S(1)}, f32[96,128]{1,0:T(8,128)S(1)}, u32[]{:S(2)}, u32[]{:S(2)}) collective-permute-start(f32[96,128]{1,0:T(8,128)S(1)} %bitcast.17), channel_id=1, source_target_pairs={{0,28},{4,8},{8,4},{12,16},{16,12},{20,24},{24,20},{28,0},{1,29},{... | collective-permute-start | bytes 147464 | tf_op jit(solution)/shard_map/ppermute | solution.py:395
  12.8 4.1 %collective-permute-start = (f32[104,128]{1,0:T(8,128)S(1)}, f32[104,128]{1,0:T(8,128)S(1)}, u32[]{:S(2)}, u32[]{:S(2)}) collective-permute-start(f32[104,128]{1,0:T(8,128)S(1)} %pad_maximum_fusion.1), channel_id=1, source_target_pairs={{0,4},{4,0},{8,12},{12,8},{16,20},{20,16},{24,28},{28,24},{1,5},{5... | collective-permute-start | bytes 159752 | tf_op jit(solution)/shard_map/ppermute | solution.py:390
  16.9 1.4 %collective-permute-start.2 = (f32[104,128]{1,0:T(8,128)S(1)}, f32[104,128]{1,0:T(8,128)S(1)}, u32[]{:S(2)}, u32[]{:S(2)}) collective-permute-start(f32[104,128]{1,0:T(8,128)S(1)} %pad_maximum_fusion.2), channel_id=1, source_target_pairs={{0,1},{1,0},{2,3},{3,2},{4,5},{5,4},{6,7},{7,6},{8,9},{9,8},{10,11... | collective-permute-start | bytes 159752 | tf_op jit(solution)/shard_map/ppermute | solution.py:390
  18.4 3.7 %collective-permute-start.3 = (f32[104,128]{1,0:T(8,128)S(1)}, f32[104,128]{1,0:T(8,128)S(1)}, u32[]{:S(2)}, u32[]{:S(2)}) collective-permute-start(f32[104,128]{1,0:T(8,128)S(1)} %pad_maximum_fusion.3), channel_id=1, source_target_pairs={{0,3},{1,2},{2,1},{3,0},{4,7},{5,6},{6,5},{7,4},{8,11},{9,10},{10,... | collective-permute-start | bytes 159752 | tf_op jit(solution)/shard_map/ppermute | solution.py:395
  22.1 6.5 %collective-permute-start.4 = (f32[8,128]{1,0:T(8,128)S(1)}, f32[8,128]{1,0:T(8,128)S(1)}, u32[]{:S(2)}, u32[]{:S(2)}) collective-permute-start(f32[8,128]{1,0:T(8,128)S(1)} %slice_add_fusion.1), channel_id=1, source_target_pairs={{0,16},{4,20},{8,24},{12,28},{16,0},{20,4},{24,8},{28,12},{1,17},{... | collective-permute-start | bytes 12296 | tf_op jit(solution)/shard_map/ppermute | solution.py:390
  26.0 10.5 %collective-permute-start.7 = (f32[3,8,128]{2,1,0:T(8,128)S(1)}, f32[3,8,128]{2,1,0:T(8,128)S(1)}, u32[]{:S(2)}, u32[]{:S(2)}) collective-permute-start(f32[3,8,128]{2,1,0:T(8,128)S(1)} %get-tuple-element.38), channel_id=1, source_target_pairs={{0,1},{1,0},{2,3},{3,2},{4,5},{5,4},{6,7},{7,6},{8,9},{9,8},{10,11... | collective-permute-start | bytes 36872 | tf_op jit(solution)/shard_map/ppermute | solution.py:390
  26.2 10.3 %collective-permute-start.8 = (f32[3,8,128]{2,1,0:T(8,128)S(1)}, f32[3,8,128]{2,1,0:T(8,128)S(1)}, u32[]{:S(2)}, u32[]{:S(2)}) collective-permute-start(f32[3,8,128]{2,1,0:T(8,128)S(1)} %get-tuple-element.39), channel_id=1, source_target_pairs={{0,3},{1,2},{2,1},{3,0},{4,7},{5,6},{6,5},{7,4},{8,11},{9,10},{10,... | collective-permute-start | bytes 36872 | tf_op jit(solution)/shard_map/ppermute | solution.py:395
  26.3 10.1 %collective-permute-start.6 = (f32[192,128]{1,0:T(8,128)S(1)}, f32[192,128]{1,0:T(8,128)S(1)}, u32[]{:S(2)}, u32[]{:S(2)}) collective-permute-start(f32[192,128]{1,0:T(8,128)S(1)} %bitcast.15), channel_id=1, source_target_pairs={{0,4},{4,0},{8,12},{12,8},{16,20},{20,16},{24,28},{28,24},{1,5},{5... | collective-permute-start | bytes 294920 | tf_op jit(solution)/shard_map/ppermute | solution.py:390
  28.6 7.8 %collective-permute-start.5 = (f32[200,128]{1,0:T(8,128)S(1)}, f32[200,128]{1,0:T(8,128)S(1)}, u32[]{:S(2)}, u32[]{:S(2)}) collective-permute-start(f32[200,128]{1,0:T(8,128)S(1)} %pad_maximum_fusion), channel_id=1, source_target_pairs={{0,28},{4,8},{8,4},{12,16},{16,12},{20,24},{24,20},{28,0},{1,29},{... | collective-permute-start | bytes 307208 | tf_op jit(solution)/shard_map/ppermute | solution.py:395
where the time goes:
time: 39.1 us; the launch traced here: 38.9 us
  Pallas kernels  22.1 us (57%)
  starting transfers between devices  15.3 us (39%)
  between operations  0.8 us (2%)
  waiting for transfers between devices  0.64 us (2%)
    pallas_call x7, Pallas kernels, call(): pl.pallas_call(kernel, out_shape=tuple((jax.ShapeDtypeStruct(shape, dtype...  22.1 us
    ppermute x4, starting transfers between devices, swap_next(): lax.ppermute(value, axis, [(i, (i - 1 if i % 2 == 0 else i + 1) % count)...  9.86 us
    ppermute x5, starting transfers between devices, swap(): return lax.ppermute(value, axis, [(i, i ^ step) for i in range(count)])  5.4 us
  transfers between devices with their start and end apart: 9, of which 2 were waited for; matrix products, arithmetic and copies ran while one was open for 0% of the time, Pallas kernels for 35%

commit v1 on v0

--- a/solution.py
+++ b/solution.py
@@ -432,8 +432,8 @@
         [pltpu.SemaphoreType.DMA((10,)), pltpu.SMEM((1, 1, 9), jnp.int32), ints(72), ints(8), ints(32)],
         flops=5 * 10**9,
     )
-    low = swap(jnp.concatenate([far[0:3].reshape(96, 128), rotor], axis=0), "gx", 1)
-    high = swap_next(far[3:6].reshape(96, 128), "gx")
+    low = swap(far[0:3].reshape(96, 128), "gx", 1)
+    high = swap_next(jnp.concatenate([far[3:6].reshape(96, 128), rotor], axis=0), "gx")
     own, acc = call(
         make_near_gather(count_y, 8, 4),
         "near_gather",
@@ -443,7 +443,7 @@
         [ints(48), ints(8)],
         flops=4 * 10**9,
     )
-    rotor = rotor + low[96:]
+    rotor = rotor + high[96:]
     own = own.reshape(96, 128)
 
     def y_payload(t):
@@ -487,8 +487,9 @@
         [pltpu.VMEM((144, 512), F32), pltpu.VMEM((3, 4, 8, 128), F32), ints(48), ints(8)],
         flops=4 * 10**9,
     )
-    xb = swap_next(jnp.concatenate([xb.reshape(192, 128), rotor], axis=0), "gx")
-    xa = swap(xa.reshape(192, 128), "gx", 1)
+    xb = swap_next(xb.reshape(192, 128), "gx")
+    rotor, ya, yb = lax.optimization_barrier((rotor, ya, yb))
+    xa = swap(jnp.concatenate([xa.reshape(192, 128), rotor], axis=0), "gx", 1)
     ya = swap(ya, "gy", 1)
     yb = swap_next(yb, "gy")
     (inner,) = call(
@@ -500,7 +501,8 @@
         [pltpu.VMEM((384, 512), F32), lists, ints(96), ints(8)],
         flops=6 * 10**9,
     )
-    rotor = rotor + xb[192:]
+    xa, xb, ya, yb = lax.optimization_barrier((xa, xb, ya, yb))
+    rotor = rotor + xa[192:]
     updated, forcing = call(
         make_stencil(count_y),
         "stencil",

time: 39.1 us -> 38.5 us (0.985)
  starting transfers between devices: 15.3 us -> 14.5 us
  waiting for transfers between devices: 0.64 us -> 0.1 us
  Pallas kernels: 22.1 us -> 22.5 us
    ppermute x5, starting transfers between devices: 5.4 us -> 3.29 us  [swap(): return lax.ppermute(value, axis, [(i, i ^ step) for i in range(count)])]
    ppermute x4, starting transfers between devices: 9.86 us -> 11.2 us  [swap_next(): lax.ppermute(value, axis, [(i, (i - 1 if i % 2 == 0 else i + 1) % count)...]
    ppermute x5, waiting for transfers between devices: 0.43 us -> 0.01 us  [swap(): return lax.ppermute(value, axis, [(i, i ^ step) for i in range(count)])]
  transfers between devices with their start and end apart: 9 -> 9, of which waited for: 2 -> 1; matrix products, arithmetic and copies ran while one was open for 0% -> 0% of each run, Pallas kernels for 35% -> 37%
where the time goes in v1:
time: 38.5 us; the launch traced here: 38 us
  Pallas kernels  22.5 us (58%)
  starting transfers between devices  14.5 us (38%)
  between operations  0.84 us (2%)
    pallas_call x7, Pallas kernels, call(): pl.pallas_call(kernel, out_shape=tuple((jax.ShapeDtypeStruct(shape, dtype...  22.5 us
    ppermute x4, starting transfers between devices, swap_next(): lax.ppermute(value, axis, [(i, (i - 1 if i % 2 == 0 else i + 1) % count)...  11.2 us
    ppermute x5, starting transfers between devices, swap(): return lax.ppermute(value, axis, [(i, i ^ step) for i in range(count)])  3.29 us
  transfers between devices with their start and end apart: 9, of which 1 were waited for; matrix products, arithmetic and copies ran while one was open for 0% of the time, Pallas kernels for 37%

profile of v1, /device:TPU:0, one launch (start us, length us, event | category | flops | bytes accessed | tf_op | source)
XLA Modules:
  0.0 38.0 jit_solution(7164874253239389370)
XLA Ops:
  0.6 6.1 %far_gather.1 = (f32[6,4,8,128]{3,2,1,0:T(8,128)S(1)}, bf16[3,256,512]{2,1,0:T(8,128)(2,1)S(1)}, f32[3,512,128]{2,1,0:T(8,128)S(1)}, s32[72,128]{1,0:T(8,128)S(1...) custom-call(s32[1]{0:T(128)} %bitcast.mine_ref, ...), custom_call_target="tpu_custom_call" | custom-call | flops 5000000000 | bytes 100000 | tf_op jit(solution)/shard_map/far_gather/pallas_call | solution.py:399
  6.7 1.3 %collective-permute-start = (f32[96,128]{1,0:T(8,128)S(1)}, f32[96,128]{1,0:T(8,128)S(1)}, u32[]{:S(2)}, u32[]{:S(2)}) collective-permute-start(f32[96,128]{1,0:T(8,128)S(1)} %bitcast.17), channel_id=1, source_target_pairs={{0,4},{4,0},{8,12},{12,8},{16,20},{20,16},{24,28},{28,24},{1,5},{5... | collective-permute-start | bytes 147464 | tf_op jit(solution)/shard_map/ppermute | solution.py:390
  8.1 5.5 %collective-permute-start.1 = (f32[104,128]{1,0:T(8,128)S(1)}, f32[104,128]{1,0:T(8,128)S(1)}, u32[]{:S(2)}, u32[]{:S(2)}) collective-permute-start(f32[104,128]{1,0:T(8,128)S(1)} %pad_maximum_fusion.1), channel_id=1, source_target_pairs={{0,28},{4,8},{8,4},{12,16},{16,12},{20,24},{24,20},{28,0},{1,29},{... | collective-permute-start | bytes 159752 | tf_op jit(solution)/shard_map/ppermute | solution.py:395
  13.5 2.2 %near_gather.1 = (f32[3,4,8,128]{3,2,1,0:T(8,128)S(1)}, f32[512,512]{1,0:T(8,128)S(1)}) custom-call(s32[1]{0:T(128)} %bitcast.mine_ref, bf16[3,256,512]{2,1,0:T(8,128)(2,1)S(1)} %get-tuple-element.29.table, s32[72,128]{1,0:T(8,128)S(1)} %get-tuple-element.30.src_ref, f32[72,128]{1,0:T(8,128)S(1)} %get-tuple-element.31.w_ref, ...), custom_call_target="tpu_custom_call" | custom-call | flops 4000000000 | bytes 100000 | tf_op jit(solution)/shard_map/near_gather/pallas_call | solution.py:399
  15.7 0.0 collective-permute-done.low_ref
  15.7 0.0 collective-permute-done.1.high_ref
  15.8 0.1 collective-permute-start.2
  15.9 1.8 %level_edges.1.base_ref = f32[144,512]{1,0:T(8,128)S(1)} custom-call(s32[1]{0:T(128)} %bitcast.mine_ref, f32[512,512]{1,0:T(8,128)S(1)} %get-tuple-element.33.base_ref, f32[96,128]{1,0:T(8,128)S(1)} %collective-permute-done.low_ref, f32[104,128]{1,0:T(8,128)S(1)} %collective-permute-done.1.high_ref, s32[72,128]{1,0:T(8,128)S(1)} %get-tuple-element.32.dst_ref), custom_call_target="tpu_custom_call" | custom-call | flops 4000000000 | bytes 100000 | tf_op jit(solution)/shard_map/level_edges/pallas_call | solution.py:399
  17.7 0.0 collective-permute-done.2.first_ref
  17.7 2.8 %collective-permute-start.3 = (f32[104,128]{1,0:T(8,128)S(1)}, f32[104,128]{1,0:T(8,128)S(1)}, u32[]{:S(2)}, u32[]{:S(2)}) collective-permute-start(f32[104,128]{1,0:T(8,128)S(1)} %pad_maximum_fusion.3), channel_id=1, source_target_pairs={{0,3},{1,2},{2,1},{3,0},{4,7},{5,6},{6,5},{7,4},{8,11},{9,10},{10,... | collective-permute-start | bytes 159752 | tf_op jit(solution)/shard_map/ppermute | solution.py:395
  20.5 1.8 %core_edges.1.base_ref = f32[144,512]{1,0:T(8,128)S(1)} custom-call(s32[1]{0:T(128)} %bitcast.mine_ref, f32[144,512]{1,0:T(8,128)S(1)} %level_edges.1.base_ref, f32[104,128]{1,0:T(8,128)S(1)} %collective-permute-done.2.first_ref, s32[72,128]{1,0:T(8,128)S(1)} %get-tuple-element.32.dst_ref), custom_call_target="tpu_custom_call" | custom-call | flops 4000000000 | bytes 100000 | tf_op jit(solution)/shard_map/core_edges/pallas_call | solution.py:399
  22.3 0.1 collective-permute-done.3.second_ref
  22.4 1.1 %collective-permute-start.4 = (f32[8,128]{1,0:T(8,128)S(1)}, f32[8,128]{1,0:T(8,128)S(1)}, u32[]{:S(2)}, u32[]{:S(2)}) collective-permute-start(f32[8,128]{1,0:T(8,128)S(1)} %slice_add_fusion), channel_id=1, source_target_pairs={{0,16},{4,20},{8,24},{12,28},{16,0},{20,4},{24,8},{28,12},{1,17},{... | collective-permute-start | bytes 12296 | tf_op jit(solution)/shard_map/ppermute | solution.py:390
  23.6 2.4 %edge_scatter.1 = (f32[3,128,128]{2,1,0:T(8,128)S(1)}, f32[3,64,128]{2,1,0:T(8,128)S(1)}, f32[3,64,128]{2,1,0:T(8,128)S(1)}, f32[3,8,128]{2,1,0:T(8,128)S(1)}, f32[3,8,128]{2,1,0:T(8,128)S(1)}) custom-call(s32[1]{0:T(128)} %bitcast.mine_ref, f32[144,512]{1,0:T(8,128)S(1)} %core_edges.1.base_ref, f32[104,128]{1,0:T(8,128)S(1)} %collective-permute-done.3.second_ref, ...), custom_call_target="tpu_custom_call" | custom-call | flops 4000000000 | bytes 100000 | tf_op jit(solution)/shard_map/edge_scatter/pallas_call | solution.py:399
  25.9 1.5 %collective-permute-start.6 = (f32[192,128]{1,0:T(8,128)S(1)}, f32[192,128]{1,0:T(8,128)S(1)}, u32[]{:S(2)}, u32[]{:S(2)}) collective-permute-start(f32[192,128]{1,0:T(8,128)S(1)} %bitcast.15), channel_id=1, source_target_pairs={{0,28},{4,8},{8,4},{12,16},{16,12},{20,24},{24,20},{28,0},{1,29},{... | collective-permute-start | bytes 294920 | tf_op jit(solution)/shard_map/ppermute | solution.py:395
  27.5 0.0 collective-permute-done.4
  27.5 0.7 %collective-permute-start.7 = (f32[3,8,128]{2,1,0:T(8,128)S(1)}, f32[3,8,128]{2,1,0:T(8,128)S(1)}, u32[]{:S(2)}, u32[]{:S(2)}) collective-permute-start(f32[3,8,128]{2,1,0:T(8,128)S(1)} %get-tuple-element.48), channel_id=1, source_target_pairs={{0,1},{1,0},{2,3},{3,2},{4,5},{5,4},{6,7},{7,6},{8,9},{9,8},{10,11... | collective-permute-start | bytes 36872 | tf_op jit(solution)/shard_map/ppermute | solution.py:390
  28.2 1.5 %collective-permute-start.8 = (f32[3,8,128]{2,1,0:T(8,128)S(1)}, f32[3,8,128]{2,1,0:T(8,128)S(1)}, u32[]{:S(2)}, u32[]{:S(2)}) collective-permute-start(f32[3,8,128]{2,1,0:T(8,128)S(1)} %get-tuple-element.49), channel_id=1, source_target_pairs={{0,3},{1,2},{2,1},{3,0},{4,7},{5,6},{6,5},{7,4},{8,11},{9,10},{10,... | collective-permute-start | bytes 36872 | tf_op jit(solution)/shard_map/ppermute | solution.py:395
  29.7 0.1 collective-permute-start.5
  29.7 5.8 %inner_scatter.1.inner_ref = f32[3,384,128]{2,1,0:T(8,128)S(1)} custom-call(s32[1]{0:T(128)} %bitcast.mine_ref, f32[512,512]{1,0:T(8,128)S(1)} %get-tuple-element.33.base_ref, f32[96,128]{1,0:T(8,128)S(1)} %collective-permute-done.low_ref, f32[104,128]{1,0:T(8,128)S(1)} %collective-permute-done.1.high_ref, f32[104,128]{1,0:T(8,128)S(1)} %collective-permute-done.2.first_ref, ...), custom_call_target="tpu_custom_call" | custom-call | flops 6000000000 | bytes 100000 | tf_op jit(solution)/shard_map/inner_scatter/pallas_call | solution.py:399
  35.5 0.0 collective-permute-done.7.ya_ref
  35.6 0.0 collective-permute-done.8.yb_ref
  35.6 0.0 collective-permute-done.6.xb_ref
  35.6 0.0 collective-permute-done.5.xa_ref
  35.6 2.4 %stencil.1 = (f32[3,8,64,128]{3,2,1,0:T(8,128)}, f32[3,512,128]{2,1,0:T(8,128)}) custom-call(s32[1]{0:T(128)} %bitcast.mine_ref, f32[3,128,128]{2,1,0:T(8,128)S(1)} %get-tuple-element.38.edge_ref, f32[3,384,128]{2,1,0:T(8,128)S(1)} %inner_scatter.1.inner_ref, s32[20,192]{1,0:T(8,128)S(1)} %get-tuple-element.39.tile_ref, ...), custom_call_target="tpu_custom_call" | custom-call | flops 1000000000 | bytes 100000 | tf_op jit(solution)/shard_map/stencil/pallas_call | solution.py:399
  (13 shorter events, 0.1 us)
Async XLA Ops:
  6.7 9.0 %collective-permute-start = (f32[96,128]{1,0:T(8,128)S(1)}, f32[96,128]{1,0:T(8,128)S(1)}, u32[]{:S(2)}, u32[]{:S(2)}) collective-permute-start(f32[96,128]{1,0:T(8,128)S(1)} %bitcast.17), channel_id=1, source_target_pairs={{0,4},{4,0},{8,12},{12,8},{16,20},{20,16},{24,28},{28,24},{1,5},{5... | collective-permute-start | bytes 147464 | tf_op jit(solution)/shard_map/ppermute | solution.py:390
  8.1 7.7 %collective-permute-start.1 = (f32[104,128]{1,0:T(8,128)S(1)}, f32[104,128]{1,0:T(8,128)S(1)}, u32[]{:S(2)}, u32[]{:S(2)}) collective-permute-start(f32[104,128]{1,0:T(8,128)S(1)} %pad_maximum_fusion.1), channel_id=1, source_target_pairs={{0,28},{4,8},{8,4},{12,16},{16,12},{20,24},{24,20},{28,0},{1,29},{... | collective-permute-start | bytes 159752 | tf_op jit(solution)/shard_map/ppermute | solution.py:395
  15.8 1.9 %collective-permute-start.2 = (f32[104,128]{1,0:T(8,128)S(1)}, f32[104,128]{1,0:T(8,128)S(1)}, u32[]{:S(2)}, u32[]{:S(2)}) collective-permute-start(f32[104,128]{1,0:T(8,128)S(1)} %pad_maximum_fusion.2), channel_id=1, source_target_pairs={{0,1},{1,0},{2,3},{3,2},{4,5},{5,4},{6,7},{7,6},{8,9},{9,8},{10,11... | collective-permute-start | bytes 159752 | tf_op jit(solution)/shard_map/ppermute | solution.py:390
  17.7 4.7 %collective-permute-start.3 = (f32[104,128]{1,0:T(8,128)S(1)}, f32[104,128]{1,0:T(8,128)S(1)}, u32[]{:S(2)}, u32[]{:S(2)}) collective-permute-start(f32[104,128]{1,0:T(8,128)S(1)} %pad_maximum_fusion.3), channel_id=1, source_target_pairs={{0,3},{1,2},{2,1},{3,0},{4,7},{5,6},{6,5},{7,4},{8,11},{9,10},{10,... | collective-permute-start | bytes 159752 | tf_op jit(solution)/shard_map/ppermute | solution.py:395
  22.4 5.0 %collective-permute-start.4 = (f32[8,128]{1,0:T(8,128)S(1)}, f32[8,128]{1,0:T(8,128)S(1)}, u32[]{:S(2)}, u32[]{:S(2)}) collective-permute-start(f32[8,128]{1,0:T(8,128)S(1)} %slice_add_fusion), channel_id=1, source_target_pairs={{0,16},{4,20},{8,24},{12,28},{16,0},{20,4},{24,8},{28,12},{1,17},{... | collective-permute-start | bytes 12296 | tf_op jit(solution)/shard_map/ppermute | solution.py:390
  25.9 9.6 %collective-permute-start.6 = (f32[192,128]{1,0:T(8,128)S(1)}, f32[192,128]{1,0:T(8,128)S(1)}, u32[]{:S(2)}, u32[]{:S(2)}) collective-permute-start(f32[192,128]{1,0:T(8,128)S(1)} %bitcast.15), channel_id=1, source_target_pairs={{0,28},{4,8},{8,4},{12,16},{16,12},{20,24},{24,20},{28,0},{1,29},{... | collective-permute-start | bytes 294920 | tf_op jit(solution)/shard_map/ppermute | solution.py:395
  27.5 8.1 %collective-permute-start.7 = (f32[3,8,128]{2,1,0:T(8,128)S(1)}, f32[3,8,128]{2,1,0:T(8,128)S(1)}, u32[]{:S(2)}, u32[]{:S(2)}) collective-permute-start(f32[3,8,128]{2,1,0:T(8,128)S(1)} %get-tuple-element.48), channel_id=1, source_target_pairs={{0,1},{1,0},{2,3},{3,2},{4,5},{5,4},{6,7},{7,6},{8,9},{9,8},{10,11... | collective-permute-start | bytes 36872 | tf_op jit(solution)/shard_map/ppermute | solution.py:390
  28.2 7.4 %collective-permute-start.8 = (f32[3,8,128]{2,1,0:T(8,128)S(1)}, f32[3,8,128]{2,1,0:T(8,128)S(1)}, u32[]{:S(2)}, u32[]{:S(2)}) collective-permute-start(f32[3,8,128]{2,1,0:T(8,128)S(1)} %get-tuple-element.49), channel_id=1, source_target_pairs={{0,3},{1,2},{2,1},{3,0},{4,7},{5,6},{6,5},{7,4},{8,11},{9,10},{10,... | collective-permute-start | bytes 36872 | tf_op jit(solution)/shard_map/ppermute | solution.py:395
  29.7 5.9 %collective-permute-start.5 = (f32[200,128]{1,0:T(8,128)S(1)}, f32[200,128]{1,0:T(8,128)S(1)}, u32[]{:S(2)}, u32[]{:S(2)}) collective-permute-start(f32[200,128]{1,0:T(8,128)S(1)} %pad_maximum_fusion), channel_id=1, source_target_pairs={{0,4},{4,0},{8,12},{12,8},{16,20},{20,16},{24,28},{28,24},{1,5},{5... | collective-permute-start | bytes 307208 | tf_op jit(solution)/shard_map/ppermute | solution.py:390

commit v2 on v1

--- a/solution.py
+++ b/solution.py
@@ -432,7 +432,7 @@
         [pltpu.SemaphoreType.DMA((10,)), pltpu.SMEM((1, 1, 9), jnp.int32), ints(72), ints(8), ints(32)],
         flops=5 * 10**9,
     )
-    low = swap(far[0:3].reshape(96, 128), "gx", 1)
+    low = swap(jnp.concatenate([far[0:3].reshape(96, 128), rotor, rotor], axis=0), "gx", 1)
     high = swap_next(jnp.concatenate([far[3:6].reshape(96, 128), rotor], axis=0), "gx")
     own, acc = call(
         make_near_gather(count_y, 8, 4),

time: 38.5 us -> 39.8 us (1.034); the launches traced: 38 us -> 40 us
  starting transfers between devices: 14.5 us -> 9.36 us
  waiting for transfers between devices: 0.1 us -> 4.68 us
  Pallas kernels: 22.5 us -> 25 us
    ppermute x5, starting transfers between devices: 3.29 us -> 0.7 us  [swap(): return lax.ppermute(value, axis, [(i, i ^ step) for i in range(count)])]
    ppermute x4, starting transfers between devices: 11.2 us -> 8.66 us  [swap_next(): lax.ppermute(value, axis, [(i, (i - 1 if i % 2 == 0 else i + 1) % count)...]
    pallas_call x7, Pallas kernels: 22.5 us -> 25 us  [call(): pl.pallas_call(kernel, out_shape=tuple((jax.ShapeDtypeStruct(shape, dtype...]
    ppermute x5, waiting for transfers between devices: 0.01 us -> 2.42 us  [swap(): return lax.ppermute(value, axis, [(i, i ^ step) for i in range(count)])]
    ppermute x4, waiting for transfers between devices: 0.09 us -> 2.26 us  [swap_next(): lax.ppermute(value, axis, [(i, (i - 1 if i % 2 == 0 else i + 1) % count)...]
  transfers between devices with their start and end apart: 9 -> 9, of which waited for: 1 -> 3; matrix products, arithmetic and copies ran while one was open for 0% -> 0% of each run, Pallas kernels for 37% -> 34%
where the time goes in v2:
time: 39.8 us; the launch traced here: 40 us
  Pallas kernels  25 us (63%)
  starting transfers between devices  9.36 us (24%)
  waiting for transfers between devices  4.68 us (12%)
  between operations  0.82 us (2%)
    pallas_call x7, Pallas kernels, call(): pl.pallas_call(kernel, out_shape=tuple((jax.ShapeDtypeStruct(shape, dtype...  25 us
    ppermute x4, starting transfers between devices, swap_next(): lax.ppermute(value, axis, [(i, (i - 1 if i % 2 == 0 else i + 1) % count)...  8.66 us
    ppermute x5, waiting for transfers between devices, swap(): return lax.ppermute(value, axis, [(i, i ^ step) for i in range(count)])  2.42 us
    ppermute x4, waiting for transfers between devices, swap_next(): lax.ppermute(value, axis, [(i, (i - 1 if i % 2 == 0 else i + 1) % count)...  2.26 us
  transfers between devices with their start and end apart: 9, of which 3 were waited for; matrix products, arithmetic and copies ran while one was open for 0% of the time, Pallas kernels for 34%

profile of v2, /device:TPU:0, one launch (start us, length us, event | category | flops | bytes accessed | tf_op | source)
XLA Modules:
  0.0 40.0 jit_solution(3301806397414907383)
XLA Ops:
  0.6 7.6 %far_gather.1 = (f32[6,4,8,128]{3,2,1,0:T(8,128)S(1)}, bf16[3,256,512]{2,1,0:T(8,128)(2,1)S(1)}, f32[3,512,128]{2,1,0:T(8,128)S(1)}, s32[72,128]{1,0:T(8,128)S(1...) custom-call(s32[1]{0:T(128)} %bitcast.mine_ref, ...), custom_call_target="tpu_custom_call" | custom-call | flops 5000000000 | bytes 100000 | tf_op jit(solution)/shard_map/far_gather/pallas_call | solution.py:399
  8.2 6.2 %collective-permute-start.1 = (f32[104,128]{1,0:T(8,128)S(1)}, f32[104,128]{1,0:T(8,128)S(1)}, u32[]{:S(2)}, u32[]{:S(2)}) collective-permute-start(f32[104,128]{1,0:T(8,128)S(1)} %pad_maximum_fusion.2), channel_id=1, source_target_pairs={{0,28},{4,8},{8,4},{12,16},{16,12},{20,24},{24,20},{28,0},{1,29},{... | collective-permute-start | bytes 159752 | tf_op jit(solution)/shard_map/ppermute | solution.py:395
  14.4 0.0 collective-permute-start
  14.4 4.5 %near_gather.1 = (f32[3,4,8,128]{3,2,1,0:T(8,128)S(1)}, f32[512,512]{1,0:T(8,128)S(1)}) custom-call(s32[1]{0:T(128)} %bitcast.mine_ref, bf16[3,256,512]{2,1,0:T(8,128)(2,1)S(1)} %get-tuple-element.29.table, s32[72,128]{1,0:T(8,128)S(1)} %get-tuple-element.30.src_ref, f32[72,128]{1,0:T(8,128)S(1)} %get-tuple-element.31.w_ref, ...), custom_call_target="tpu_custom_call" | custom-call | flops 4000000000 | bytes 100000 | tf_op jit(solution)/shard_map/near_gather/pallas_call | solution.py:399
  18.9 0.0 collective-permute-done.1.high_ref
  18.9 0.0 collective-permute-done.low_ref
  19.0 0.1 collective-permute-start.2
  19.0 1.8 %level_edges.1.base_ref = f32[144,512]{1,0:T(8,128)S(1)} custom-call(s32[1]{0:T(128)} %bitcast.mine_ref, f32[512,512]{1,0:T(8,128)S(1)} %get-tuple-element.33.base_ref, f32[112,128]{1,0:T(8,128)S(1)} %collective-permute-done.low_ref, f32[104,128]{1,0:T(8,128)S(1)} %collective-permute-done.1.high_ref, s32[72,128]{1,0:T(8,128)S(1)} %get-tuple-element.32.dst_ref), custom_call_target="tpu_custom_call" | custom-call | flops 4000000000 | bytes 100000 | tf_op jit(solution)/shard_map/level_edges/pallas_call | solution.py:399
  20.9 0.0 collective-permute-done.2.first_ref
  20.9 0.6 %collective-permute-start.3 = (f32[104,128]{1,0:T(8,128)S(1)}, f32[104,128]{1,0:T(8,128)S(1)}, u32[]{:S(2)}, u32[]{:S(2)}) collective-permute-start(f32[104,128]{1,0:T(8,128)S(1)} %pad_maximum_fusion.4), channel_id=1, source_target_pairs={{0,3},{1,2},{2,1},{3,0},{4,7},{5,6},{6,5},{7,4},{8,11},{9,10},{10,... | collective-permute-start | bytes 159752 | tf_op jit(solution)/shard_map/ppermute | solution.py:395
  21.5 1.3 %core_edges.1.base_ref = f32[144,512]{1,0:T(8,128)S(1)} custom-call(s32[1]{0:T(128)} %bitcast.mine_ref, f32[144,512]{1,0:T(8,128)S(1)} %level_edges.1.base_ref, f32[104,128]{1,0:T(8,128)S(1)} %collective-permute-done.2.first_ref, s32[72,128]{1,0:T(8,128)S(1)} %get-tuple-element.32.dst_ref), custom_call_target="tpu_custom_call" | custom-call | flops 4000000000 | bytes 100000 | tf_op jit(solution)/shard_map/core_edges/pallas_call | solution.py:399
  22.8 2.3 %collective-permute-done.3.second_ref = f32[104,128]{1,0:T(8,128)S(1)} collective-permute-done((f32[104,128]{1,0:T(8,128)S(1)}, f32[104,128]{1,0:T(8,128)S(1)}, u32[]{:S(2)}, u32[]{:S(2)}) %collective-permute-start.3) | collective-permute-done | bytes 53280 | tf_op jit(solution)/shard_map/ppermute | solution.py:395
  25.1 0.0 collective-permute-start.4
  25.1 1.4 %edge_scatter.1 = (f32[3,128,128]{2,1,0:T(8,128)S(1)}, f32[3,64,128]{2,1,0:T(8,128)S(1)}, f32[3,64,128]{2,1,0:T(8,128)S(1)}, f32[3,8,128]{2,1,0:T(8,128)S(1)}, f32[3,8,128]{2,1,0:T(8,128)S(1)}) custom-call(s32[1]{0:T(128)} %bitcast.mine_ref, f32[144,512]{1,0:T(8,128)S(1)} %core_edges.1.base_ref, f32[104,128]{1,0:T(8,128)S(1)} %collective-permute-done.3.second_ref, ...), custom_call_target="tpu_custom_call" | custom-call | flops 4000000000 | bytes 100000 | tf_op jit(solution)/shard_map/edge_scatter/pallas_call | solution.py:399
  26.5 1.6 %collective-permute-start.6 = (f32[192,128]{1,0:T(8,128)S(1)}, f32[192,128]{1,0:T(8,128)S(1)}, u32[]{:S(2)}, u32[]{:S(2)}) collective-permute-start(f32[192,128]{1,0:T(8,128)S(1)} %bitcast.15), channel_id=1, source_target_pairs={{0,28},{4,8},{8,4},{12,16},{16,12},{20,24},{24,20},{28,0},{1,29},{... | collective-permute-start | bytes 294920 | tf_op jit(solution)/shard_map/ppermute | solution.py:395
  28.1 1.5 %collective-permute-done.4 = f32[8,128]{1,0:T(8,128)S(1)} collective-permute-done((f32[8,128]{1,0:T(8,128)S(1)}, f32[8,128]{1,0:T(8,128)S(1)}, u32[]{:S(2)}, u32[]{:S(2)}) %collective-permute-start.4) | collective-permute-done | bytes 4128 | tf_op jit(solution)/shard_map/ppermute | solution.py:390
  29.6 0.0 collective-permute-start.7
  29.6 0.4 collective-permute-start.8
  30.0 0.6 %collective-permute-start.5 = (f32[200,128]{1,0:T(8,128)S(1)}, f32[200,128]{1,0:T(8,128)S(1)}, u32[]{:S(2)}, u32[]{:S(2)}) collective-permute-start(f32[200,128]{1,0:T(8,128)S(1)} %pad_maximum_fusion), channel_id=1, source_target_pairs={{0,4},{4,0},{8,12},{12,8},{16,20},{20,16},{24,28},{28,24},{1,5},{5... | collective-permute-start | bytes 307208 | tf_op jit(solution)/shard_map/ppermute | solution.py:390
  30.6 4.6 %inner_scatter.1.inner_ref = f32[3,384,128]{2,1,0:T(8,128)S(1)} custom-call(s32[1]{0:T(128)} %bitcast.mine_ref, f32[512,512]{1,0:T(8,128)S(1)} %get-tuple-element.33.base_ref, f32[112,128]{1,0:T(8,128)S(1)} %collective-permute-done.low_ref, f32[104,128]{1,0:T(8,128)S(1)} %collective-permute-done.1.high_ref, f32[104,128]{1,0:T(8,128)S(1)} %collective-permute-done.2.first_ref, ...), custom_call_target="tpu_custom_call" | custom-call | flops 6000000000 | bytes 100000 | tf_op jit(solution)/shard_map/inner_scatter/pallas_call | solution.py:399
  35.2 0.0 collective-permute-done.7.ya_ref
  35.2 0.0 collective-permute-done.8.yb_ref
  35.2 0.0 collective-permute-done.6.xb_ref
  35.2 0.9 %collective-permute-done.5.xa_ref = f32[200,128]{1,0:T(8,128)S(1)} collective-permute-done((f32[200,128]{1,0:T(8,128)S(1)}, f32[200,128]{1,0:T(8,128)S(1)}, u32[]{:S(2)}, u32[]{:S(2)}) %collective-permute-start.5) | collective-permute-done | bytes 102432 | tf_op jit(solution)/shard_map/ppermute | solution.py:390
  36.1 3.9 %stencil.1 = (f32[3,8,64,128]{3,2,1,0:T(8,128)}, f32[3,512,128]{2,1,0:T(8,128)}) custom-call(s32[1]{0:T(128)} %bitcast.mine_ref, f32[3,128,128]{2,1,0:T(8,128)S(1)} %get-tuple-element.38.edge_ref, f32[3,384,128]{2,1,0:T(8,128)S(1)} %inner_scatter.1.inner_ref, s32[20,192]{1,0:T(8,128)S(1)} %get-tuple-element.39.tile_ref, ...), custom_call_target="tpu_custom_call" | custom-call | flops 1000000000 | bytes 100000 | tf_op jit(solution)/shard_map/stencil/pallas_call | solution.py:399
  (14 shorter events, 0.1 us)
Async XLA Ops:
  8.2 10.7 %collective-permute-start.1 = (f32[104,128]{1,0:T(8,128)S(1)}, f32[104,128]{1,0:T(8,128)S(1)}, u32[]{:S(2)}, u32[]{:S(2)}) collective-permute-start(f32[104,128]{1,0:T(8,128)S(1)} %pad_maximum_fusion.2), channel_id=1, source_target_pairs={{0,28},{4,8},{8,4},{12,16},{16,12},{20,24},{24,20},{28,0},{1,29},{... | collective-permute-start | bytes 159752 | tf_op jit(solution)/shard_map/ppermute | solution.py:395
  14.4 4.5 %collective-permute-start = (f32[112,128]{1,0:T(8,128)S(1)}, f32[112,128]{1,0:T(8,128)S(1)}, u32[]{:S(2)}, u32[]{:S(2)}) collective-permute-start(f32[112,128]{1,0:T(8,128)S(1)} %pad_maximum_fusion.1), channel_id=1, source_target_pairs={{0,4},{4,0},{8,12},{12,8},{16,20},{20,16},{24,28},{28,24},{1,5},{5... | collective-permute-start | bytes 172040 | tf_op jit(solution)/shard_map/ppermute | solution.py:390
  19.0 1.9 %collective-permute-start.2 = (f32[104,128]{1,0:T(8,128)S(1)}, f32[104,128]{1,0:T(8,128)S(1)}, u32[]{:S(2)}, u32[]{:S(2)}) collective-permute-start(f32[104,128]{1,0:T(8,128)S(1)} %pad_maximum_fusion.3), channel_id=1, source_target_pairs={{0,1},{1,0},{2,3},{3,2},{4,5},{5,4},{6,7},{7,6},{8,9},{9,8},{10,11... | collective-permute-start | bytes 159752 | tf_op jit(solution)/shard_map/ppermute | solution.py:390
  20.9 4.2 %collective-permute-start.3 = (f32[104,128]{1,0:T(8,128)S(1)}, f32[104,128]{1,0:T(8,128)S(1)}, u32[]{:S(2)}, u32[]{:S(2)}) collective-permute-start(f32[104,128]{1,0:T(8,128)S(1)} %pad_maximum_fusion.4), channel_id=1, source_target_pairs={{0,3},{1,2},{2,1},{3,0},{4,7},{5,6},{6,5},{7,4},{8,11},{9,10},{10,... | collective-permute-start | bytes 159752 | tf_op jit(solution)/shard_map/ppermute | solution.py:395
  25.1 4.5 %collective-permute-start.4 = (f32[8,128]{1,0:T(8,128)S(1)}, f32[8,128]{1,0:T(8,128)S(1)}, u32[]{:S(2)}, u32[]{:S(2)}) collective-permute-start(f32[8,128]{1,0:T(8,128)S(1)} %slice_add_fusion), channel_id=1, source_target_pairs={{0,16},{4,20},{8,24},{12,28},{16,0},{20,4},{24,8},{28,12},{1,17},{... | collective-permute-start | bytes 12296 | tf_op jit(solution)/shard_map/ppermute | solution.py:390
  26.5 8.7 %collective-permute-start.6 = (f32[192,128]{1,0:T(8,128)S(1)}, f32[192,128]{1,0:T(8,128)S(1)}, u32[]{:S(2)}, u32[]{:S(2)}) collective-permute-start(f32[192,128]{1,0:T(8,128)S(1)} %bitcast.15), channel_id=1, source_target_pairs={{0,28},{4,8},{8,4},{12,16},{16,12},{20,24},{24,20},{28,0},{1,29},{... | collective-permute-start | bytes 294920 | tf_op jit(solution)/shard_map/ppermute | solution.py:395
  29.6 5.6 %collective-permute-start.7 = (f32[3,8,128]{2,1,0:T(8,128)S(1)}, f32[3,8,128]{2,1,0:T(8,128)S(1)}, u32[]{:S(2)}, u32[]{:S(2)}) collective-permute-start(f32[3,8,128]{2,1,0:T(8,128)S(1)} %get-tuple-element.48), channel_id=1, source_target_pairs={{0,1},{1,0},{2,3},{3,2},{4,5},{5,4},{6,7},{7,6},{8,9},{9,8},{10,11... | collective-permute-start | bytes 36872 | tf_op jit(solution)/shard_map/ppermute | solution.py:390
  29.6 5.6 %collective-permute-start.8 = (f32[3,8,128]{2,1,0:T(8,128)S(1)}, f32[3,8,128]{2,1,0:T(8,128)S(1)}, u32[]{:S(2)}, u32[]{:S(2)}) collective-permute-start(f32[3,8,128]{2,1,0:T(8,128)S(1)} %get-tuple-element.49), channel_id=1, source_target_pairs={{0,3},{1,2},{2,1},{3,0},{4,7},{5,6},{6,5},{7,4},{8,11},{9,10},{10,... | collective-permute-start | bytes 36872 | tf_op jit(solution)/shard_map/ppermute | solution.py:395
  30.0 6.1 %collective-permute-start.5 = (f32[200,128]{1,0:T(8,128)S(1)}, f32[200,128]{1,0:T(8,128)S(1)}, u32[]{:S(2)}, u32[]{:S(2)}) collective-permute-start(f32[200,128]{1,0:T(8,128)S(1)} %pad_maximum_fusion), channel_id=1, source_target_pairs={{0,4},{4,0},{8,12},{12,8},{16,20},{20,16},{24,28},{28,24},{1,5},{5... | collective-permute-start | bytes 307208 | tf_op jit(solution)/shard_map/ppermute | solution.py:390

commit v3 on v2

--- a/solution.py
+++ b/solution.py
@@ -435,7 +435,7 @@
     low = swap(jnp.concatenate([far[0:3].reshape(96, 128), rotor, rotor], axis=0), "gx", 1)
     high = swap_next(jnp.concatenate([far[3:6].reshape(96, 128), rotor], axis=0), "gx")
     own, acc = call(
-        make_near_gather(count_y, 8, 4),
+        make_near_gather(count_y, 12, 4),
         "near_gather",
         [((3, 4, 8, 128), F32, VMEM), ((512, 512), F32, VMEM)],
         [SMEM] + [VMEM] * 4,

time: 39.8 us -> 38.1 us (0.957); the launches traced: 40 us -> 37.5 us
  starting transfers between devices: 9.36 us -> 12.9 us
  Pallas kernels: 25 us -> 21.8 us
  waiting for transfers between devices: 4.68 us -> 1.97 us
    pallas_call x7, Pallas kernels: 25 us -> 21.8 us  [call(): pl.pallas_call(kernel, out_shape=tuple((jax.ShapeDtypeStruct(shape, dtype...]
    ppermute x4, starting transfers between devices: 8.66 us -> 11.2 us  [swap_next(): lax.ppermute(value, axis, [(i, (i - 1 if i % 2 == 0 else i + 1) % count)...]
    ppermute x4, waiting for transfers between devices: 2.26 us -> 0.89 us  [swap_next(): lax.ppermute(value, axis, [(i, (i - 1 if i % 2 == 0 else i + 1) % count)...]
    ppermute x5, waiting for transfers between devices: 2.42 us -> 1.08 us  [swap(): return lax.ppermute(value, axis, [(i, i ^ step) for i in range(count)])]
    ppermute x5, starting transfers between devices: 0.7 us -> 1.69 us  [swap(): return lax.ppermute(value, axis, [(i, i ^ step) for i in range(count)])]
  transfers between devices with their start and end apart: 9 -> 9, of which waited for: 3 -> 4; matrix products, arithmetic and copies ran while one was open for 0% -> 0% of each run, Pallas kernels for 34% -> 34%
where the time goes in v3:
time: 38.1 us; the launch traced here: 37.5 us
  Pallas kernels  21.8 us (57%)
  starting transfers between devices  12.9 us (34%)
  waiting for transfers between devices  1.97 us (5%)
  between operations  0.78 us (2%)
    pallas_call x7, Pallas kernels, call(): pl.pallas_call(kernel, out_shape=tuple((jax.ShapeDtypeStruct(shape, dtype...  21.8 us
    ppermute x4, starting transfers between devices, swap_next(): lax.ppermute(value, axis, [(i, (i - 1 if i % 2 == 0 else i + 1) % count)...  11.2 us
    ppermute x5, starting transfers between devices, swap(): return lax.ppermute(value, axis, [(i, i ^ step) for i in range(count)])  1.69 us
    ppermute x5, waiting for transfers between devices, swap(): return lax.ppermute(value, axis, [(i, i ^ step) for i in range(count)])  1.08 us
    ppermute x4, waiting for transfers between devices, swap_next(): lax.ppermute(value, axis, [(i, (i - 1 if i % 2 == 0 else i + 1) % count)...  0.89 us
  transfers between devices with their start and end apart: 9, of which 4 were waited for; matrix products, arithmetic and copies ran while one was open for 0% of the time, Pallas kernels for 34%

profile of v3, /device:TPU:0, one launch (start us, length us, event | category | flops | bytes accessed | tf_op | source)
XLA Modules:
  0.0 37.5 jit_solution(8022475356726021812)
XLA Ops:
  0.6 6.7 %far_gather.1 = (f32[6,4,8,128]{3,2,1,0:T(8,128)S(1)}, bf16[3,256,512]{2,1,0:T(8,128)(2,1)S(1)}, f32[3,512,128]{2,1,0:T(8,128)S(1)}, s32[72,128]{1,0:T(8,128)S(1...) custom-call(s32[1]{0:T(128)} %bitcast.mine_ref, ...), custom_call_target="tpu_custom_call" | custom-call | flops 5000000000 | bytes 100000 | tf_op jit(solution)/shard_map/far_gather/pallas_call | solution.py:399
  7.4 6.0 %collective-permute-start.1 = (f32[104,128]{1,0:T(8,128)S(1)}, f32[104,128]{1,0:T(8,128)S(1)}, u32[]{:S(2)}, u32[]{:S(2)}) collective-permute-start(f32[104,128]{1,0:T(8,128)S(1)} %pad_maximum_fusion.2), channel_id=1, source_target_pairs={{0,28},{4,8},{8,4},{12,16},{16,12},{20,24},{24,20},{28,0},{1,29},{... | collective-permute-start | bytes 159752 | tf_op jit(solution)/shard_map/ppermute | solution.py:395
  13.4 0.0 collective-permute-start
  13.4 3.9 %near_gather.1 = (f32[3,4,8,128]{3,2,1,0:T(8,128)S(1)}, f32[512,512]{1,0:T(8,128)S(1)}) custom-call(s32[1]{0:T(128)} %bitcast.mine_ref, bf16[3,256,512]{2,1,0:T(8,128)(2,1)S(1)} %get-tuple-element.29.table, s32[72,128]{1,0:T(8,128)S(1)} %get-tuple-element.30.src_ref, f32[72,128]{1,0:T(8,128)S(1)} %get-tuple-element.31.w_ref, ...), custom_call_target="tpu_custom_call" | custom-call | flops 4000000000 | bytes 100000 | tf_op jit(solution)/shard_map/near_gather/pallas_call | solution.py:399
  17.4 0.0 collective-permute-done.1.high_ref
  17.4 0.2 collective-permute-done.low_ref
  17.6 0.1 collective-permute-start.2
  17.7 1.1 %level_edges.1.base_ref = f32[144,512]{1,0:T(8,128)S(1)} custom-call(s32[1]{0:T(128)} %bitcast.mine_ref, f32[512,512]{1,0:T(8,128)S(1)} %get-tuple-element.33.base_ref, f32[112,128]{1,0:T(8,128)S(1)} %collective-permute-done.low_ref, f32[104,128]{1,0:T(8,128)S(1)} %collective-permute-done.1.high_ref, s32[72,128]{1,0:T(8,128)S(1)} %get-tuple-element.32.dst_ref), custom_call_target="tpu_custom_call" | custom-call | flops 4000000000 | bytes 100000 | tf_op jit(solution)/shard_map/level_edges/pallas_call | solution.py:399
  18.9 0.1 collective-permute-done.2.first_ref
  18.9 1.4 %collective-permute-start.3 = (f32[104,128]{1,0:T(8,128)S(1)}, f32[104,128]{1,0:T(8,128)S(1)}, u32[]{:S(2)}, u32[]{:S(2)}) collective-permute-start(f32[104,128]{1,0:T(8,128)S(1)} %pad_maximum_fusion.4), channel_id=1, source_target_pairs={{0,3},{1,2},{2,1},{3,0},{4,7},{5,6},{6,5},{7,4},{8,11},{9,10},{10,... | collective-permute-start | bytes 159752 | tf_op jit(solution)/shard_map/ppermute | solution.py:395
  20.3 1.3 %core_edges.1.base_ref = f32[144,512]{1,0:T(8,128)S(1)} custom-call(s32[1]{0:T(128)} %bitcast.mine_ref, f32[144,512]{1,0:T(8,128)S(1)} %level_edges.1.base_ref, f32[104,128]{1,0:T(8,128)S(1)} %collective-permute-done.2.first_ref, s32[72,128]{1,0:T(8,128)S(1)} %get-tuple-element.32.dst_ref), custom_call_target="tpu_custom_call" | custom-call | flops 4000000000 | bytes 100000 | tf_op jit(solution)/shard_map/core_edges/pallas_call | solution.py:399
  21.7 0.9 %collective-permute-done.3.second_ref = f32[104,128]{1,0:T(8,128)S(1)} collective-permute-done((f32[104,128]{1,0:T(8,128)S(1)}, f32[104,128]{1,0:T(8,128)S(1)}, u32[]{:S(2)}, u32[]{:S(2)}) %collective-permute-start.3) | collective-permute-done | bytes 53280 | tf_op jit(solution)/shard_map/ppermute | solution.py:395
  22.6 1.0 %collective-permute-start.4 = (f32[8,128]{1,0:T(8,128)S(1)}, f32[8,128]{1,0:T(8,128)S(1)}, u32[]{:S(2)}, u32[]{:S(2)}) collective-permute-start(f32[8,128]{1,0:T(8,128)S(1)} %slice_add_fusion), channel_id=1, source_target_pairs={{0,16},{4,20},{8,24},{12,28},{16,0},{20,4},{24,8},{28,12},{1,17},{... | collective-permute-start | bytes 12296 | tf_op jit(solution)/shard_map/ppermute | solution.py:390
  23.6 1.9 %edge_scatter.1 = (f32[3,128,128]{2,1,0:T(8,128)S(1)}, f32[3,64,128]{2,1,0:T(8,128)S(1)}, f32[3,64,128]{2,1,0:T(8,128)S(1)}, f32[3,8,128]{2,1,0:T(8,128)S(1)}, f32[3,8,128]{2,1,0:T(8,128)S(1)}) custom-call(s32[1]{0:T(128)} %bitcast.mine_ref, f32[144,512]{1,0:T(8,128)S(1)} %core_edges.1.base_ref, f32[104,128]{1,0:T(8,128)S(1)} %collective-permute-done.3.second_ref, ...), custom_call_target="tpu_custom_call" | custom-call | flops 4000000000 | bytes 100000 | tf_op jit(solution)/shard_map/edge_scatter/pallas_call | solution.py:399
  25.5 2.7 %collective-permute-start.6 = (f32[192,128]{1,0:T(8,128)S(1)}, f32[192,128]{1,0:T(8,128)S(1)}, u32[]{:S(2)}, u32[]{:S(2)}) collective-permute-start(f32[192,128]{1,0:T(8,128)S(1)} %bitcast.15), channel_id=1, source_target_pairs={{0,28},{4,8},{8,4},{12,16},{16,12},{20,24},{24,20},{28,0},{1,29},{... | collective-permute-start | bytes 294920 | tf_op jit(solution)/shard_map/ppermute | solution.py:395
  28.1 0.0 collective-permute-done.4
  28.2 0.0 collective-permute-start.7
  28.2 1.1 %collective-permute-start.8 = (f32[3,8,128]{2,1,0:T(8,128)S(1)}, f32[3,8,128]{2,1,0:T(8,128)S(1)}, u32[]{:S(2)}, u32[]{:S(2)}) collective-permute-start(f32[3,8,128]{2,1,0:T(8,128)S(1)} %get-tuple-element.49), channel_id=1, source_target_pairs={{0,3},{1,2},{2,1},{3,0},{4,7},{5,6},{6,5},{7,4},{8,11},{9,10},{10,... | collective-permute-start | bytes 36872 | tf_op jit(solution)/shard_map/ppermute | solution.py:395
  29.3 0.6 %collective-permute-start.5 = (f32[200,128]{1,0:T(8,128)S(1)}, f32[200,128]{1,0:T(8,128)S(1)}, u32[]{:S(2)}, u32[]{:S(2)}) collective-permute-start(f32[200,128]{1,0:T(8,128)S(1)} %pad_maximum_fusion), channel_id=1, source_target_pairs={{0,4},{4,0},{8,12},{12,8},{16,20},{20,16},{24,28},{28,24},{1,5},{5... | collective-permute-start | bytes 307208 | tf_op jit(solution)/shard_map/ppermute | solution.py:390
  29.9 4.4 %inner_scatter.1.inner_ref = f32[3,384,128]{2,1,0:T(8,128)S(1)} custom-call(s32[1]{0:T(128)} %bitcast.mine_ref, f32[512,512]{1,0:T(8,128)S(1)} %get-tuple-element.33.base_ref, f32[112,128]{1,0:T(8,128)S(1)} %collective-permute-done.low_ref, f32[104,128]{1,0:T(8,128)S(1)} %collective-permute-done.1.high_ref, f32[104,128]{1,0:T(8,128)S(1)} %collective-permute-done.2.first_ref, ...), custom_call_target="tpu_custom_call" | custom-call | flops 6000000000 | bytes 100000 | tf_op jit(solution)/shard_map/inner_scatter/pallas_call | solution.py:399
  34.3 0.0 collective-permute-done.7.ya_ref
  34.3 0.0 collective-permute-done.8.yb_ref
  34.3 0.0 collective-permute-done.6.xb_ref
  34.3 0.8 %collective-permute-done.5.xa_ref = f32[200,128]{1,0:T(8,128)S(1)} collective-permute-done((f32[200,128]{1,0:T(8,128)S(1)}, f32[200,128]{1,0:T(8,128)S(1)}, u32[]{:S(2)}, u32[]{:S(2)}) %collective-permute-start.5) | collective-permute-done | bytes 102432 | tf_op jit(solution)/shard_map/ppermute | solution.py:390
  35.1 2.4 %stencil.1 = (f32[3,8,64,128]{3,2,1,0:T(8,128)}, f32[3,512,128]{2,1,0:T(8,128)}) custom-call(s32[1]{0:T(128)} %bitcast.mine_ref, f32[3,128,128]{2,1,0:T(8,128)S(1)} %get-tuple-element.38.edge_ref, f32[3,384,128]{2,1,0:T(8,128)S(1)} %inner_scatter.1.inner_ref, s32[20,192]{1,0:T(8,128)S(1)} %get-tuple-element.39.tile_ref, ...), custom_call_target="tpu_custom_call" | custom-call | flops 1000000000 | bytes 100000 | tf_op jit(solution)/shard_map/stencil/pallas_call | solution.py:399
  (14 shorter events, 0.1 us)
Async XLA Ops:
  7.4 10.0 %collective-permute-start.1 = (f32[104,128]{1,0:T(8,128)S(1)}, f32[104,128]{1,0:T(8,128)S(1)}, u32[]{:S(2)}, u32[]{:S(2)}) collective-permute-start(f32[104,128]{1,0:T(8,128)S(1)} %pad_maximum_fusion.2), channel_id=1, source_target_pairs={{0,28},{4,8},{8,4},{12,16},{16,12},{20,24},{24,20},{28,0},{1,29},{... | collective-permute-start | bytes 159752 | tf_op jit(solution)/shard_map/ppermute | solution.py:395
  13.4 4.2 %collective-permute-start = (f32[112,128]{1,0:T(8,128)S(1)}, f32[112,128]{1,0:T(8,128)S(1)}, u32[]{:S(2)}, u32[]{:S(2)}) collective-permute-start(f32[112,128]{1,0:T(8,128)S(1)} %pad_maximum_fusion.1), channel_id=1, source_target_pairs={{0,4},{4,0},{8,12},{12,8},{16,20},{20,16},{24,28},{28,24},{1,5},{5... | collective-permute-start | bytes 172040 | tf_op jit(solution)/shard_map/ppermute | solution.py:390
  17.6 1.3 %collective-permute-start.2 = (f32[104,128]{1,0:T(8,128)S(1)}, f32[104,128]{1,0:T(8,128)S(1)}, u32[]{:S(2)}, u32[]{:S(2)}) collective-permute-start(f32[104,128]{1,0:T(8,128)S(1)} %pad_maximum_fusion.3), channel_id=1, source_target_pairs={{0,1},{1,0},{2,3},{3,2},{4,5},{5,4},{6,7},{7,6},{8,9},{9,8},{10,11... | collective-permute-start | bytes 159752 | tf_op jit(solution)/shard_map/ppermute | solution.py:390
  18.9 3.6 %collective-permute-start.3 = (f32[104,128]{1,0:T(8,128)S(1)}, f32[104,128]{1,0:T(8,128)S(1)}, u32[]{:S(2)}, u32[]{:S(2)}) collective-permute-start(f32[104,128]{1,0:T(8,128)S(1)} %pad_maximum_fusion.4), channel_id=1, source_target_pairs={{0,3},{1,2},{2,1},{3,0},{4,7},{5,6},{6,5},{7,4},{8,11},{9,10},{10,... | collective-permute-start | bytes 159752 | tf_op jit(solution)/shard_map/ppermute | solution.py:395
  22.6 5.6 %collective-permute-start.4 = (f32[8,128]{1,0:T(8,128)S(1)}, f32[8,128]{1,0:T(8,128)S(1)}, u32[]{:S(2)}, u32[]{:S(2)}) collective-permute-start(f32[8,128]{1,0:T(8,128)S(1)} %slice_add_fusion), channel_id=1, source_target_pairs={{0,16},{4,20},{8,24},{12,28},{16,0},{20,4},{24,8},{28,12},{1,17},{... | collective-permute-start | bytes 12296 | tf_op jit(solution)/shard_map/ppermute | solution.py:390
  25.5 8.8 %collective-permute-start.6 = (f32[192,128]{1,0:T(8,128)S(1)}, f32[192,128]{1,0:T(8,128)S(1)}, u32[]{:S(2)}, u32[]{:S(2)}) collective-permute-start(f32[192,128]{1,0:T(8,128)S(1)} %bitcast.15), channel_id=1, source_target_pairs={{0,28},{4,8},{8,4},{12,16},{16,12},{20,24},{24,20},{28,0},{1,29},{... | collective-permute-start | bytes 294920 | tf_op jit(solution)/shard_map/ppermute | solution.py:395
  28.2 6.1 %collective-permute-start.7 = (f32[3,8,128]{2,1,0:T(8,128)S(1)}, f32[3,8,128]{2,1,0:T(8,128)S(1)}, u32[]{:S(2)}, u32[]{:S(2)}) collective-permute-start(f32[3,8,128]{2,1,0:T(8,128)S(1)} %get-tuple-element.48), channel_id=1, source_target_pairs={{0,1},{1,0},{2,3},{3,2},{4,5},{5,4},{6,7},{7,6},{8,9},{9,8},{10,11... | collective-permute-start | bytes 36872 | tf_op jit(solution)/shard_map/ppermute | solution.py:390
  28.2 6.1 %collective-permute-start.8 = (f32[3,8,128]{2,1,0:T(8,128)S(1)}, f32[3,8,128]{2,1,0:T(8,128)S(1)}, u32[]{:S(2)}, u32[]{:S(2)}) collective-permute-start(f32[3,8,128]{2,1,0:T(8,128)S(1)} %get-tuple-element.49), channel_id=1, source_target_pairs={{0,3},{1,2},{2,1},{3,0},{4,7},{5,6},{6,5},{7,4},{8,11},{9,10},{10,... | collective-permute-start | bytes 36872 | tf_op jit(solution)/shard_map/ppermute | solution.py:395
  29.3 5.8 %collective-permute-start.5 = (f32[200,128]{1,0:T(8,128)S(1)}, f32[200,128]{1,0:T(8,128)S(1)}, u32[]{:S(2)}, u32[]{:S(2)}) collective-permute-start(f32[200,128]{1,0:T(8,128)S(1)} %pad_maximum_fusion), channel_id=1, source_target_pairs={{0,4},{4,0},{8,12},{12,8},{16,20},{20,16},{24,28},{28,24},{1,5},{5... | collective-permute-start | bytes 307208 | tf_op jit(solution)/shard_map/ppermute | solution.py:390
